TPU v7x, 128 devices: a whole 4x4x4 slice. The times are simulated.
128 devices in a mesh: grp: 4 (over z_lo, core), dev: 32 (over z_hi, x, y).
Axes of the slice: x: 4, y: 4, z: 4 (z_hi: 2, z_lo: 2; z = z_hi * 2 + z_lo), core: 2. Of those that a mesh axis runs over, the one named last changes fastest.
Arguments:
- fine_residual: bfloat16 [4, 32, 4, 4, 24, 2, 3072], P('grp', 'dev'), may hold values from -4 to 4
- near_null: bfloat16 [4, 32, 4, 4, 2, 32, 3072], P('grp', 'dev'), may hold values from -0.375 to 0.375
- coarse_operator: bfloat16 [4, 32, 4, 4, 64, 1152], P(None, 'dev'), may hold values from -1 to 7
Outputs:
- fine_correction: bfloat16 [4, 32, 4, 4, 24, 2, 3072], P('grp', 'dev')
- coarse_residual: float32 [4, 32, 4, 4, 24, 128], P('grp', 'dev')
All inputs are finite; a program needn't handle non-finite values.
Results may differ from a plain program's by a relative error of at most 0.012.
The roundings to bfloat16 on the way count: a program that leaves them out, or rounds other values in their place, can miss the bound.
Values may be sent and summed in bfloat16 or wider, within the bound.
A program may use at most 128 MiB of HBM per device.

v0:
```python
import jax
import jax.numpy as jnp
from jax import lax
from jax.sharding import PartitionSpec as P

ITERS = 3


def padded_2(block, sides, width):
    for axis, dim in sides:
        count = lax.axis_size(axis)
        forward = [(i, i + 1) for i in range(count - 1)]
        forward.append((count - 1, 0))
        backward = [(target, source) for source, target in forward]
        low = lax.ppermute(
            lax.slice_in_dim(block, block.shape[dim] - width, None, axis=dim), axis, forward
        )
        high = lax.ppermute(lax.slice_in_dim(block, 0, width, axis=dim), axis, backward)
        block = jnp.concatenate([low, block, high], axis=dim)
    return block


def complex_columns(piece, ncoarse):
    real_part = piece[..., :ncoarse]
    imag_part = piece[..., ncoarse:]
    former = jnp.concatenate([real_part, -imag_part], axis=-1)
    latter = jnp.concatenate([imag_part, real_part], axis=-1)
    return jnp.stack([former, latter], axis=-2)


def restrict_local(vectors, field):
    middle = vectors.shape[-1] // 2
    upper = jnp.einsum(
        "tzyxpkm,tzyxnqm->tzyxnpqk",
        vectors[..., :middle],
        field[..., :middle],
        preferred_element_type=jnp.float32,
    )
    lower = jnp.einsum(
        "tzyxpkm,tzyxnqm->tzyxnpqk",
        vectors[..., middle:],
        field[..., middle:],
        preferred_element_type=jnp.float32,
    )
    joined = jnp.concatenate([upper, lower], axis=-1)
    real_part = joined[..., 0, 0, :] + joined[..., 1, 1, :]
    imag_part = joined[..., 0, 1, :] - joined[..., 1, 0, :]
    return jnp.concatenate([real_part, imag_part], axis=-1)


def coefficients(solution, first_index, last_index, ncoarse):
    real_part = solution[..., first_index:last_index]
    imag_part = solution[..., ncoarse + first_index : ncoarse + last_index]
    former = jnp.stack([real_part, -imag_part], axis=-2)
    latter = jnp.stack([imag_part, real_part], axis=-2)
    return jnp.stack([former, latter], axis=-3)


def prolong_local(vectors, rounded):
    vector_count = vectors.shape[-2]
    ncoarse = 2 * vector_count
    middle = vectors.shape[-1] // 2
    upper = jnp.einsum(
        "tzyxnqpk,tzyxpkm->tzyxnqm",
        coefficients(rounded, 0, vector_count, ncoarse),
        vectors[..., :middle],
        preferred_element_type=jnp.float32,
    )
    lower = jnp.einsum(
        "tzyxnqpk,tzyxpkm->tzyxnqm",
        coefficients(rounded, vector_count, ncoarse, ncoarse),
        vectors[..., middle:],
        preferred_element_type=jnp.float32,
    )
    return jnp.concatenate([upper, lower], axis=-1).astype(jnp.bfloat16)


def coarse_apply(operator, rounded, ncoarse):
    padded = padded_2(rounded, (("dev", 1),), 1)
    centre = padded[:, 1:-1]
    next_time = jnp.roll(centre, -1, 0)
    prev_time = jnp.roll(centre, 1, 0)
    next_depth = padded[:, 2:]
    prev_depth = padded[:, :-2]
    shifted = [
        centre,
        next_time,
        prev_time,
        next_depth,
        prev_depth,
        jnp.roll(centre, -1, 2),
        jnp.roll(centre, 1, 2),
        jnp.roll(centre, -1, 3),
        jnp.roll(centre, 1, 3),
    ]
    columns = complex_columns(jnp.stack(shifted, axis=4), ncoarse)
    leading = centre.shape[:4]
    sites_total = leading[0] * leading[1] * leading[2] * leading[3]
    blocks = operator.reshape(sites_total, ncoarse, 9, 2 * ncoarse)
    columns = columns.reshape((sites_total,) + columns.shape[4:])
    result = jnp.einsum("sidk,sdnqk->snqi", blocks, columns, preferred_element_type=jnp.float32)
    return result.reshape(leading + (result.shape[1], 2 * ncoarse))


def reduce_terms(terms):
    return lax.psum(terms, "dev")


def inner_terms(left, right, ncoarse):
    left_re = left[..., :ncoarse]
    left_im = left[..., ncoarse:]
    right_re = right[..., :ncoarse]
    right_im = right[..., ncoarse:]
    summed = (0, 1, 2, 3, 5)
    return jnp.stack(
        [
            jnp.sum(left_re * right_re + left_im * right_im, axis=summed),
            jnp.sum(left_re * right_im - left_im * right_re, axis=summed),
        ]
    )


def scaled(coef, vector, ncoarse):
    coef_real = coef[0][:, None]
    coef_imag = coef[1][:, None]
    vec_real = vector[..., :ncoarse]
    vec_imag = vector[..., ncoarse:]
    return jnp.concatenate(
        [coef_real * vec_real - coef_imag * vec_imag, coef_real * vec_imag + coef_imag * vec_real],
        axis=-1,
    )


def solve_coarse(source, operator, ncoarse):
    solution = jnp.zeros_like(source)
    residual = source
    directions = []
    images = []
    curvatures = []
    for iteration in range(ITERS):
        direction = residual
        product = coarse_apply(operator, direction.astype(jnp.bfloat16), ncoarse)
        if iteration > 0:
            correlations = reduce_terms(
                jnp.stack([inner_terms(earlier_q, product, ncoarse) for earlier_q in images])
            )
            for earlier in range(iteration):
                factor = correlations[earlier] / curvatures[earlier][None, :]
                product = product - scaled(factor, images[earlier], ncoarse)
                direction = direction - scaled(factor, directions[earlier], ncoarse)
        totals = reduce_terms(
            jnp.stack(
                [inner_terms(product, product, ncoarse), inner_terms(product, residual, ncoarse)]
            )
        )
        curvature = totals[0, 0]
        along = totals[1]
        step_size = along / curvature[None, :]
        solution = solution + scaled(step_size, direction, ncoarse)
        residual = residual - scaled(step_size, product, ncoarse)
        directions.append(direction)
        images.append(product)
        curvatures.append(curvature)
    return (solution, residual)


def on_device(fine_residual, near_null, coarse_operator):
    ncoarse = 2 * near_null.shape[-2]
    planes = fine_residual.shape[0]
    restricted = restrict_local(near_null, fine_residual)
    source = lax.all_gather(restricted, "grp", axis=0, tiled=True)
    solution, residual = solve_coarse(source, coarse_operator, ncoarse)
    offset = lax.axis_index("grp") * planes
    own_solution = lax.dynamic_slice_in_dim(solution, offset, planes, 0)
    own_residual = lax.dynamic_slice_in_dim(residual, offset, planes, 0)
    fine_correction = prolong_local(near_null, own_solution.astype(jnp.bfloat16))
    return (fine_correction, own_residual)


def solution(mesh):
    in_specs = (
        P("grp", "dev", None, None, None, None, None),
        P("grp", "dev", None, None, None, None, None),
        P(None, "dev", None, None, None, None),
    )
    out_specs = (
        P("grp", "dev", None, None, None, None, None),
        P("grp", "dev", None, None, None, None),
    )
    return jax.shard_map(
        on_device, mesh=mesh, in_specs=in_specs, out_specs=out_specs, check_vma=False
    )
```

profile of v0, /device:TPU:0, one launch (start us, length us, event | category | flops | bytes accessed | tf_op | source)
XLA Modules:
  0.0 667.4 jit_solution(16897455706575244473)
XLA Ops:
  0.6 6.3 fusion.95
  7.0 2.7 fusion.37
  9.7 2.7 fusion.40
  12.8 9.1 %all_gather.3 = f32[4,1,4,4,24,128]{5,4,3,2,1,0:T(8,128)S(1)} all-gather(f32[1,1,4,4,24,128]{5,4,3,2,1,0:T(8,128)S(1)} %pad_maximum_fusion.8), channel_id=1, replica_groups=mesh['grp'=4,'dev'=32] {'grp'}, dimensions={0}, use_global_device_ids=true | all-gather | bytes 983040 | tf_op jit(solution)/shard_map/all_gather | solution.py:171
  22.0 0.9 bitcast_dynamic-update-slice_fusion.8
  22.9 8.2 %collective-permute-start = (bf16[4,1,4,4,24,128]{5,4,3,2,0,1:T(8,128)(2,1)S(1)}, bf16[4,1,4,4,24,128]{5,4,3,2,0,1:T(8,128)(2,1)S(1)}, u32[]{:S(2)}, u32[]{:S(2)}) collective-permute-start(bf16[4,1,4,4,24,128]{5,4,3,2,0,1:T(8,128)(2,1)S(1)} %bitcast.357), channel_id=1, source_target_pairs={{1,0},{2,1},{3,2},{4,3},{5,4},{6,5},{7,6},{8,7},{9,8},{10,9},{11,1... | collective-permute-start | bytes 1179656 | tf_op jit(solution)/shard_map/ppermute | solution.py:18
  31.3 0.7 fusion.106
  32.7 0.8 fusion.45
  33.6 0.7 slice.457
  34.9 19.7 %reshape.360 = bf16[64,64,9,128]{3,2,1,0:T(8,128)(2,1)} reshape(bf16[4,1,4,4,64,1152]{5,4,3,2,1,0:T(8,128)(2,1)} %param.5) | data formatting | bytes 18874368 | tf_op jit(solution)/shard_map/reshape | solution.py:99
  54.6 1.7 fusion.46
  56.3 0.8 bitcast_dynamic-update-slice_fusion.7
  57.1 0.8 bitcast_dynamic-update-slice_fusion.6
  57.9 1.7 fusion.47
  59.6 0.8 fusion.48
  60.4 0.8 fusion.49
  61.2 0.8 fusion.50
  62.0 3.9 slice_negate_fusion.2
  65.9 3.9 pad_maximum_fusion.1
  69.8 2.4 copy.184
  72.2 2.4 copy.185
  74.6 12.1 %fusion.34 = f32[64,24,2,64]{3,1,2,0:T(8,128)} fusion(bf16[64,9,24,1,128]{4,2,1,3,0:T(8,128)(2,1)} %bitcast.392, bf16[64,9,24,1,128]{4,2,1,3,0:T(8,128)(2,1)} %bitcast.389, bf16[64,64,9,128,1]{3,2,1,0,4:T(8,128)(2,1)} %bitcast.381), kind=kOutput, calls=%fused_computation.37 | convolution fusion | flops 456523776 | bytes 17301504 | tf_op jit(solution)/shard_map/sidk,sdnqk->snqi/dot_general | solution.py:101
  86.7 2.2 copy.187
  88.9 0.9 reshape.361
  89.8 0.7 add_reduce_fusion.7
  90.5 96.6 %psum.35 = f32[2,2,24]{2,1,0:T(2,128)S(1)} all-reduce(f32[2,2,24]{2,1,0:T(2,128)S(1)} %pad_maximum_fusion.9), channel_id=1, replica_groups=mesh['grp'=4,'dev'=32] {'dev'}, use_global_device_ids=true, to_apply=%region_4.5 | all-reduce | flops 96 | bytes 768 | tf_op jit(solution)/shard_map/psum | solution.py:106
  188.4 2.0 collective-permute-start.3
  190.8 5.4 collective-permute-done.2
  196.3 5.7 collective-permute-done.3
  202.4 1.5 slice_negate_fusion.1
  203.9 3.9 pad_maximum_fusion.3
  207.9 2.4 copy.202
  210.3 2.4 copy.203
  212.7 12.1 %fusion.31 = f32[64,24,2,64]{3,1,2,0:T(8,128)} fusion(bf16[64,9,24,1,128]{4,2,1,3,0:T(8,128)(2,1)} %bitcast.393, bf16[64,9,24,1,128]{4,2,1,3,0:T(8,128)(2,1)} %bitcast.390, bf16[64,64,9,128,1]{3,2,1,0,4:T(8,128)(2,1)} %bitcast.382), kind=kOutput, calls=%fused_computation.36 | convolution fusion | flops 456523776 | bytes 17301504 | tf_op jit(solution)/shard_map/sidk,sdnqk->snqi/dot_general | solution.py:101
  224.8 3.4 copy.205
  228.1 2.3 reshape.362
  231.1 89.0 %psum.36 = f32[2,24]{1,0:T(2,128)S(1)} all-reduce(f32[2,24]{1,0:T(2,128)S(1)} %pad_maximum_fusion.13), channel_id=1, replica_groups=mesh['grp'=4,'dev'=32] {'dev'}, use_global_device_ids=true, to_apply=%region_7.8 | all-reduce | flops 48 | bytes 384 | tf_op jit(solution)/shard_map/psum | solution.py:106
  320.5 1.4 maximum_subtract_fusion.1
  321.9 0.7 add_reduce_fusion.4
  322.6 90.9 %psum.37 = f32[2,2,24]{2,1,0:T(2,128)S(1)} all-reduce(f32[2,2,24]{2,1,0:T(2,128)S(1)} %pad_maximum_fusion.10), channel_id=1, replica_groups=mesh['grp'=4,'dev'=32] {'dev'}, use_global_device_ids=true, to_apply=%region_12.13 | all-reduce | flops 96 | bytes 768 | tf_op jit(solution)/shard_map/psum | solution.py:106
  413.9 1.2 bitcast_dynamic-update-slice_fusion.2
  415.3 2.0 collective-permute-start.5
  417.7 5.5 collective-permute-done.4
  423.2 5.7 collective-permute-done.5
  429.3 1.5 slice_negate_fusion
  430.9 3.9 pad_maximum_fusion.5
  434.8 2.4 copy.221
  437.2 2.4 copy.222
  439.6 12.1 %fusion.28 = f32[64,24,2,64]{3,1,2,0:T(8,128)} fusion(bf16[64,9,24,1,128]{4,2,1,3,0:T(8,128)(2,1)} %bitcast.391, bf16[64,9,24,1,128]{4,2,1,3,0:T(8,128)(2,1)} %bitcast.388, bf16[64,64,9,128,1]{3,2,1,0,4:T(8,128)(2,1)} %bitcast.383), kind=kOutput, calls=%fused_computation.35 | convolution fusion | flops 456523776 | bytes 17301504 | tf_op jit(solution)/shard_map/sidk,sdnqk->snqi/dot_general | solution.py:101
  451.7 3.4 copy.224
  455.1 3.0 reshape.363
  458.1 2.2 add_reduce_fusion.3
  460.3 89.1 %psum.38 = f32[2,2,24]{2,1,0:T(2,128)S(1)} all-reduce(f32[2,2,24]{2,1,0:T(2,128)S(1)} %pad_maximum_fusion.11), channel_id=1, replica_groups=mesh['grp'=4,'dev'=32] {'dev'}, use_global_device_ids=true, to_apply=%region_17.18 | all-reduce | flops 96 | bytes 768 | tf_op jit(solution)/shard_map/psum | solution.py:106
  549.4 2.3 multiply_add_fusion.11
  552.3 2.3 multiply_add_fusion.7
  555.8 0.7 add_reduce_fusion
  556.5 90.9 %psum.39 = f32[2,2,24]{2,1,0:T(2,128)S(1)} all-reduce(f32[2,2,24]{2,1,0:T(2,128)S(1)} %pad_maximum_fusion.12), channel_id=1, replica_groups=mesh['grp'=4,'dev'=32] {'dev'}, use_global_device_ids=true, to_apply=%region_22.23 | all-reduce | flops 96 | bytes 768 | tf_op jit(solution)/shard_map/psum | solution.py:106
  647.4 1.8 fusion.44
  651.1 1.0 fusion.76
  652.4 0.8 slice-done.1
  653.3 0.8 fusion.18
  654.2 0.9 fusion.21
  655.1 2.7 pad_maximum_fusion
  657.8 9.4 %copy.231 = bf16[1,1,4,4,24,2,3072]{6,5,4,3,2,1,0:T(2,128)(2,1)} copy(bf16[1,1,4,4,24,2,3072]{6,4,5,3,2,1,0:T(8,128)(2,1)} %pad_maximum_fusion) | data formatting | bytes 9437184
  (113 shorter events, 10.4 us)
Async XLA Ops:
  0.6 6.3 copy-start.3
  22.9 33.5 %collective-permute-start = (bf16[4,1,4,4,24,128]{5,4,3,2,0,1:T(8,128)(2,1)S(1)}, bf16[4,1,4,4,24,128]{5,4,3,2,0,1:T(8,128)(2,1)S(1)}, u32[]{:S(2)}, u32[]{:S(2)}) collective-permute-start(bf16[4,1,4,4,24,128]{5,4,3,2,0,1:T(8,128)(2,1)S(1)} %bitcast.357), channel_id=1, source_target_pairs={{1,0},{2,1},{3,2},{4,3},{5,4},{6,5},{7,6},{8,7},{9,8},{10,9},{11,1... | collective-permute-start | bytes 1179656 | tf_op jit(solution)/shard_map/ppermute | solution.py:18
  31.1 26.0 %collective-permute-start.1 = (bf16[4,1,4,4,24,128]{5,4,3,2,0,1:T(8,128)(2,1)S(1)}, bf16[4,1,4,4,24,128]{5,4,3,2,0,1:T(8,128)(2,1)S(1)}, u32[]{:S(2)}, u32[]{:S(2)}) collective-permute-start(bf16[4,1,4,4,24,128]{5,4,3,2,0,1:T(8,128)(2,1)S(1)} %bitcast.358), channel_id=1, source_target_pairs={{0,1},{1,2},{2,3},{3,4},{4,5},{5,6},{6,7},{7,8},{8,9},{9,10},{10,1... | collective-permute-start | bytes 1179656 | tf_op jit(solution)/shard_map/ppermute | solution.py:15
  54.6 5.8 copy-start.11
  54.6 6.6 copy-start.10
  188.0 8.3 %collective-permute-start.2 = (bf16[4,1,4,4,24,128]{5,4,3,2,0,1:T(8,128)(2,1)S(1)}, bf16[4,1,4,4,24,128]{5,4,3,2,0,1:T(8,128)(2,1)S(1)}, u32[]{:S(2)}, u32[]{:S(2)}) collective-permute-start(bf16[4,1,4,4,24,128]{5,4,3,2,0,1:T(8,128)(2,1)S(1)} %bitcast.367), channel_id=1, source_target_pairs={{1,0},{2,1},{3,2},{4,3},{5,4},{6,5},{7,6},{8,7},{9,8},{10,9},{11,1... | collective-permute-start | bytes 1179656 | tf_op jit(solution)/shard_map/ppermute | solution.py:18
  188.4 13.6 %collective-permute-start.3 = (bf16[4,1,4,4,24,128]{5,4,3,2,0,1:T(8,128)(2,1)S(1)}, bf16[4,1,4,4,24,128]{5,4,3,2,0,1:T(8,128)(2,1)S(1)}, u32[]{:S(2)}, u32[]{:S(2)}) collective-permute-start(bf16[4,1,4,4,24,128]{5,4,3,2,0,1:T(8,128)(2,1)S(1)} %bitcast.368), channel_id=1, source_target_pairs={{0,1},{1,2},{2,3},{3,4},{4,5},{5,6},{6,7},{7,8},{8,9},{9,10},{10,1... | collective-permute-start | bytes 1179656 | tf_op jit(solution)/shard_map/ppermute | solution.py:15
  230.5 90.0 %copy-start.2 = (f32[4,1,4,4,24,128]{5,4,3,2,0,1:T(8,128)}, f32[4,1,4,4,24,128]{5,4,3,2,0,1:T(8,128)S(1)}, u32[]{:S(2)}) copy-start(f32[4,1,4,4,24,128]{5,4,3,2,0,1:T(8,128)S(1)} %reshape.362) | copy-start | bytes 2359300
  415.2 7.9 %collective-permute-start.4 = (bf16[4,1,4,4,24,128]{5,4,3,2,0,1:T(8,128)(2,1)S(1)}, bf16[4,1,4,4,24,128]{5,4,3,2,0,1:T(8,128)(2,1)S(1)}, u32[]{:S(2)}, u32[]{:S(2)}) collective-permute-start(bf16[4,1,4,4,24,128]{5,4,3,2,0,1:T(8,128)(2,1)S(1)} %bitcast.375), channel_id=1, source_target_pairs={{1,0},{2,1},{3,2},{4,3},{5,4},{6,5},{7,6},{8,7},{9,8},{10,9},{11,1... | collective-permute-start | bytes 1179656 | tf_op jit(solution)/shard_map/ppermute | solution.py:18
  415.3 13.7 %collective-permute-start.5 = (bf16[4,1,4,4,24,128]{5,4,3,2,0,1:T(8,128)(2,1)S(1)}, bf16[4,1,4,4,24,128]{5,4,3,2,0,1:T(8,128)(2,1)S(1)}, u32[]{:S(2)}, u32[]{:S(2)}) collective-permute-start(bf16[4,1,4,4,24,128]{5,4,3,2,0,1:T(8,128)(2,1)S(1)} %bitcast.376), channel_id=1, source_target_pairs={{0,1},{1,2},{2,3},{3,4},{4,5},{5,6},{6,7},{7,8},{8,9},{9,10},{10,1... | collective-permute-start | bytes 1179656 | tf_op jit(solution)/shard_map/ppermute | solution.py:15
  552.3 2.3 copy-start.1
  554.6 1.1 copy-start
  554.6 92.8 %copy-start.4 = (f32[4,1,4,4,24,64]{5,4,3,2,1,0:T(8,128)S(1)}, f32[4,1,4,4,24,64]{5,4,3,2,1,0:T(8,128)}, u32[]{:S(2)}) copy-start(f32[4,1,4,4,24,64]{5,4,3,2,1,0:T(8,128)} %get-tuple-element.81) | copy-start | bytes 1179652
  555.1 92.3 %copy-start.5 = (f32[4,1,4,4,24,64]{5,4,3,2,1,0:T(8,128)S(1)}, f32[4,1,4,4,24,64]{5,4,3,2,1,0:T(8,128)}, u32[]{:S(2)}) copy-start(f32[4,1,4,4,24,64]{5,4,3,2,1,0:T(8,128)} %get-tuple-element.82) | copy-start | bytes 1179652
  649.3 1.1 copy-start.6
  649.3 1.4 copy-start.7
  649.3 1.6 copy-start.8
  649.3 1.8 copy-start.9
  649.3 3.1 slice-start
  651.1 2.2 slice-start.1
where the time goes:
time: 674 us; the launch traced here: 667 us
  blocking collectives  466 us (69%)
  local copies, waits for them, and re-layouts  72.9 us (11%)
  other arithmetic  48.6 us (7%)
  matrix products  43.4 us (6%)
  waiting for transfers between devices  22.3 us (3%)
  starting transfers between devices  13 us (2%)
    psum x5, blocking collectives, reduce_terms(): return lax.psum(terms, 'dev')  456 us
    dot_general x3, matrix products, coarse_apply(): jnp.einsum('sidk,sdnqk->snqi', blocks, columns, preferred_element_type=jn...  36.3 us
    reshape x1, local copies, waits for them, and re-layouts, coarse_apply(): blocks = operator.reshape(sites_total, ncoarse, 9, 2 * ncoarse)  19.7 us
    unnamed x35, local copies, waits for them, and re-layouts  14 us
  transfers between devices with their start and end apart: 6, of which 4 were waited for; matrix products, arithmetic and copies ran while one was open for 4% of the time, Pallas kernels for 0%

commit v1 on v0

v1 whole, which is shorter than its diff:
```python
import jax
import jax.numpy as jnp
from jax import lax
from jax.experimental import pallas as pl
from jax.experimental.pallas import tpu as pltpu
from jax.sharding import PartitionSpec as P

ITERS = 3
SITES = 16
SIDE = 4
NRHS = 24
NVEC = 64
COMP = 128
FINE = 3072
HALF = FINE // 2
GRP = 4
DEV = 32
PLANE = 16
LINE = 8
GROUPS = 4
PER = SITES // GROUPS
BF = jnp.bfloat16
F32 = jnp.float32
NT = (((1,), (1,)), ((), ()))
VMEM_LIMIT = 60 * 2**20


def lanes():
    return lax.broadcasted_iota(jnp.int32, (1, COMP), 1)


def flipped(v):
    return jnp.where(lanes() < 64, 1.0, -1.0) * pltpu.roll(v, 64, 1)


def restrict_sites(cat, first):
    even = cat[pl.ds(2 * NRHS * first, NRHS * PER, stride=2), :]
    odd = cat[pl.ds(2 * NRHS * first + 1, NRHS * PER, stride=2), :]
    re = even + pltpu.roll(odd, 96, 1)
    im = odd - pltpu.roll(even, 96, 1)
    lane = lanes()
    return jnp.where(
        lane < 32,
        re,
        jnp.where(
            lane < 64,
            pltpu.roll(re, 96, 1),
            jnp.where(lane < 96, pltpu.roll(im, 64, 1), pltpu.roll(im, 32, 1)),
        ),
    )


def coefficient_rows(c):
    lane = lanes()
    r32, r64, r96 = (pltpu.roll(c, k, 1) for k in (32, 64, 96))
    real = jnp.where(lane < 32, c, jnp.where(lane < 64, -r96, jnp.where(lane < 96, r32, -c)))
    imag = jnp.where(lane < 32, r64, jnp.where(lane < 64, r32, jnp.where(lane < 96, r96, r64)))
    return real, imag


def packed(terms):
    lane = lanes()
    out = jnp.zeros((8, COMP), F32)
    for t, values in enumerate(terms):
        total = jnp.sum(values, axis=1, keepdims=True)
        for a in range(3):
            out = jnp.where(lane == 32 * a + t, total[8 * a : 8 * a + 8], out)
    return out


def unpacked(message, t):
    return message if t == 0 else pltpu.roll(message, COMP - t, 1)


def spread(coef):
    return jnp.concatenate(
        [jnp.broadcast_to(coef[:, 32 * a : 32 * a + 1], (8, COMP)) for a in range(3)], axis=0
    )


def scale(re, im):
    re, im = spread(re), spread(im)
    return lambda v: re * v - im * flipped(v)


def site(y, x):
    return (y % SIDE) * SIDE + x % SIDE


def gcr_kernel(
    f_hbm, v_hbm, op_hbm, coef_ref, out_ref,
    fb, vb, ob, wide, cat, res, first, second, sol, prod, low, halo,
    msg1, msg2, box1, box2,
    f_sem, v_sem, o_sem, h_send, h_recv, s1_send, s1_recv, s2_send, s2_recv,
):
    g = lax.axis_index("grp")
    d = lax.axis_index("dev")
    high = d // PLANE
    place = d % PLANE
    line = high * GRP + g

    def line_peer(k):
        other = (line + k) % LINE
        return {"grp": other % GRP, "dev": (other // GRP) * PLANE + place}

    def plane_peer(k):
        return {"grp": g, "dev": high * PLANE + (place + k) % PLANE}

    halo_to = [
        {"grp": (g + GRP - 1) % GRP, "dev": d},
        {"grp": (g + 1) % GRP, "dev": d},
        {"grp": g, "dev": (d + DEV - 1) % DEV},
        {"grp": g, "dev": (d + 1) % DEV},
    ]

    copies = []
    for j in range(GROUPS):
        part = pl.ds(j * PER, PER)
        pair = (
            pltpu.make_async_copy(f_hbm.at[part], fb.at[part], f_sem.at[j]),
            pltpu.make_async_copy(v_hbm.at[part], vb.at[part], v_sem.at[j]),
        )
        for copy in pair:
            copy.start()
        copies.append(pair)
    op_copy = pltpu.make_async_copy(op_hbm.at[g], ob, o_sem)
    op_copy.start()

    barrier = pltpu.get_barrier_semaphore()
    greeted = halo_to[2:] + [line_peer(k) for k in range(1, LINE)]
    greeted += [plane_peer(k) for k in range(1, PLANE)]
    for peer in greeted:
        pl.semaphore_signal(barrier, inc=1, device_id=peer, device_id_type=pl.DeviceIdType.MESH)

    for j in range(GROUPS):
        for copy in copies[j]:
            copy.wait()
        for s in range(j * PER, j * PER + PER):
            f = fb[s].reshape(2 * NRHS, FINE)
            upper = lax.dot_general(f[:, :HALF], vb[s, :, :HALF], NT, preferred_element_type=F32)
            lower = lax.dot_general(f[:, HALF:], vb[s, :, HALF:], NT, preferred_element_type=F32)
            cat[2 * NRHS * s : 2 * NRHS * (s + 1), :] = jnp.concatenate([upper, lower], axis=1)
        block = restrict_sites(cat, j * PER).reshape(PER, NRHS, COMP)
        res[0, pl.ds(j * PER, PER)] = block
        low[0, pl.ds(j * PER, PER)] = block.astype(BF)
    pl.semaphore_wait(barrier, len(greeted))

    sends = []

    def remote(src, dst, send, recv, peer):
        copy = pltpu.make_async_remote_copy(
            src_ref=src, dst_ref=dst, send_sem=send, recv_sem=recv,
            device_id=peer, device_id_type=pl.DeviceIdType.MESH,
        )
        copy.start()
        sends.append(copy)
        return copy

    def start_halo(k):
        return [
            remote(low.at[k], halo.at[k, h], h_send.at[k, h], h_recv.at[k, h], halo_to[h])
            for h in range(4)
        ]

    def widen():
        keep = jnp.where(lanes() < 64, 1.0, -1.0).astype(BF)
        for s in range(SITES):
            for c in range(9):
                block = ob[s, :, COMP * c : COMP * (c + 1)]
                wide[s, 0:64, COMP * c : COMP * (c + 1)] = block * keep
                wide[s, 64:128, COMP * c : COMP * (c + 1)] = jnp.concatenate(
                    [block[:, 64:], block[:, :64]], axis=1
                )

    def apply_own(k):
        for y in range(SIDE):
            for x in range(SIDE):
                s = site(y, x)
                near = [site(y + 1, x), site(y - 1, x), site(y, x + 1), site(y, x - 1)]
                side = jnp.concatenate([low[k, n] for n in near], axis=1)
                prod[k, s] = lax.dot_general(
                    low[k, s], wide[s, :, :COMP], NT, preferred_element_type=F32
                ) + lax.dot_general(side, wide[s, :, 5 * COMP :], NT, preferred_element_type=F32)

    def apply_halo(k):
        for s in range(SITES):
            far = jnp.concatenate([halo[k, h, s] for h in range(4)], axis=1)
            prod[k, s] += lax.dot_general(
                far, wide[s, :, COMP : 5 * COMP], NT, preferred_element_type=F32
            )

    def total(k, terms, meanwhile):
        mine = packed(terms)
        msg1[k] = mine
        arriving = [
            remote(msg1.at[k], box1.at[k, i - 1], s1_send.at[k, i - 1], s1_recv.at[k, i - 1], line_peer(i))
            for i in range(1, LINE)
        ]
        meanwhile()
        for copy in arriving:
            copy.wait_recv()
        mine = mine + jnp.sum(box1[k], axis=0)
        msg2[k] = mine
        arriving = [
            remote(msg2.at[k], box2.at[k, i - 1], s2_send.at[k, i - 1], s2_recv.at[k, i - 1], plane_peer(i))
            for i in range(1, PLANE)
        ]
        for copy in arriving:
            copy.wait_recv()
        return mine + jnp.sum(box2[k], axis=0)

    def inner(k):
        zero = jnp.zeros((NRHS, COMP), F32)
        sums = [zero] * (3 + 4 * k)
        for s in range(SITES):
            q, r = prod[k, s], res[k, s]
            iq, ir = flipped(q), flipped(r)
            new = [q * q, q * r, q * ir]
            for j in range(k):
                e = prod[j, s]
                new += [e * q, e * iq, e * r, e * ir]
            sums = [a + b for a, b in zip(sums, new)]
        return sums

    arriving = start_halo(0)
    op_copy.wait()
    widen()
    apply_own(0)
    for copy in arriving:
        copy.wait_recv()
    apply_halo(0)
    sums = total(0, inner(0), lambda: None)
    norm0 = unpacked(sums, 0)
    a0_re, a0_im = unpacked(sums, 1) / norm0, unpacked(sums, 2) / norm0
    step = scale(a0_re, a0_im)
    for s in range(SITES):
        r = res[0, s] - step(prod[0, s])
        res[1, s] = r
        low[1, s] = r.astype(BF)

    arriving = start_halo(1)
    for s in range(SITES):
        sol[s] = step(res[0, s])
    apply_own(1)
    for copy in arriving:
        copy.wait_recv()
    apply_halo(1)
    sums = total(1, inner(1), lambda: None)
    s_re, s_im = unpacked(sums, 3), unpacked(sums, 4)
    b_re, b_im = s_re / norm0, s_im / norm0
    norm1 = unpacked(sums, 0) - (b_re * s_re + b_im * s_im)
    e_re, e_im = unpacked(sums, 5), unpacked(sums, 6)
    along_re = unpacked(sums, 1) - (b_re * e_re + b_im * e_im)
    along_im = unpacked(sums, 2) - (b_re * e_im - b_im * e_re)
    back = scale(b_re, b_im)
    step = scale(along_re / norm1, along_im / norm1)
    for s in range(SITES):
        q = prod[1, s] - back(prod[0, s])
        prod[1, s] = q
        r = res[1, s] - step(q)
        res[2, s] = r
        low[2, s] = r.astype(BF)

    arriving = start_halo(2)
    for s in range(SITES):
        p = res[1, s] - back(res[0, s])
        first[s] = p
        sol[s] += step(p)
    apply_own(2)
    for copy in arriving:
        copy.wait_recv()
    apply_halo(2)
    sums = total(2, inner(2), lambda: None)
    s_re, s_im, e_re, e_im = (unpacked(sums, 3 + i) for i in range(4))
    u_re, u_im, w_re, w_im = (unpacked(sums, 7 + i) for i in range(4))
    b_re, b_im = s_re / norm0, s_im / norm0
    c_re, c_im = u_re / norm1, u_im / norm1
    norm2 = unpacked(sums, 0) - (b_re * s_re + b_im * s_im) - (c_re * u_re + c_im * u_im)
    along_re = unpacked(sums, 1) - (b_re * e_re + b_im * e_im) - (c_re * w_re + c_im * w_im)
    along_im = unpacked(sums, 2) - (b_re * e_im - b_im * e_re) - (c_re * w_im - c_im * w_re)
    back0, back1 = scale(b_re, b_im), scale(c_re, c_im)
    step = scale(along_re / norm2, along_im / norm2)
    for s in range(SITES):
        q = prod[2, s] - back0(prod[0, s]) - back1(prod[1, s])
        out_ref[s] = res[2, s] - step(q)
        p = res[2, s] - back0(res[0, s]) - back1(first[s])
        x = sol[s] + step(p)
        real, imag = coefficient_rows(x.astype(BF).astype(F32))
        second[pl.ds(2 * NRHS * s, NRHS, stride=2), :] = real
        second[pl.ds(2 * NRHS * s + 1, NRHS, stride=2), :] = imag
        coef_ref[s] = second[2 * NRHS * s : 2 * NRHS * (s + 1), :].astype(BF)
    for copy in sends:
        copy.wait_send()


def solve(fine, vectors, operator):
    any_space = pl.BlockSpec(memory_space=pl.ANY)
    in_vmem = pl.BlockSpec(memory_space=pltpu.VMEM)
    field = (SITES, NRHS, COMP)
    dma = pltpu.SemaphoreType.DMA
    return pl.pallas_call(
        gcr_kernel,
        out_shape=(
            jax.ShapeDtypeStruct((SITES, 2 * NRHS, COMP), BF),
            jax.ShapeDtypeStruct(field, F32),
        ),
        in_specs=[any_space] * 3,
        out_specs=(in_vmem, in_vmem),
        scratch_shapes=[
            pltpu.VMEM((SITES, NRHS, 2, FINE), BF),
            pltpu.VMEM((SITES, NVEC, FINE), BF),
            pltpu.VMEM((SITES, 64, 9 * COMP), BF),
            pltpu.VMEM((SITES, 128, 9 * COMP), BF),
            pltpu.VMEM((SITES * 2 * NRHS, COMP), F32),
            pltpu.VMEM((ITERS, *field), F32),
            pltpu.VMEM(field, F32),
            pltpu.VMEM((SITES * 2 * NRHS, COMP), F32),
            pltpu.VMEM(field, F32),
            pltpu.VMEM((ITERS, *field), F32),
            pltpu.VMEM((ITERS, *field), BF),
            pltpu.VMEM((ITERS, 4, *field), BF),
            pltpu.VMEM((ITERS, 8, COMP), F32),
            pltpu.VMEM((ITERS, 8, COMP), F32),
            pltpu.VMEM((ITERS, LINE - 1, 8, COMP), F32),
            pltpu.VMEM((ITERS, PLANE - 1, 8, COMP), F32),
            dma((GROUPS,)),
            dma((GROUPS,)),
            dma,
            dma((ITERS, 4)),
            dma((ITERS, 4)),
            dma((ITERS, LINE - 1)),
            dma((ITERS, LINE - 1)),
            dma((ITERS, PLANE - 1)),
            dma((ITERS, PLANE - 1)),
        ],
        compiler_params=pltpu.CompilerParams(
            collective_id=0, has_side_effects=True, vmem_limit_bytes=VMEM_LIMIT
        ),
        name="restrict_gcr",
    )(fine, vectors, operator)


def prolong_kernel(v_hbm, coef_ref, o_hbm, yb, vb, v_sem, o_sem):
    loads, stores = [], []
    for j in range(GROUPS):
        part = pl.ds(j * PER, PER)
        loads.append(pltpu.make_async_copy(v_hbm.at[part], vb.at[part], v_sem.at[j]))
        stores.append(pltpu.make_async_copy(yb.at[part], o_hbm.at[part], o_sem.at[j]))
        loads[j].start()
    for j in range(GROUPS):
        loads[j].wait()
        for s in range(j * PER, j * PER + PER):
            c = coef_ref[s]
            upper = jnp.dot(c[:, :64], vb[s, :, :HALF], preferred_element_type=F32).astype(BF)
            lower = jnp.dot(c[:, 64:], vb[s, :, HALF:], preferred_element_type=F32).astype(BF)
            yb[s] = jnp.concatenate([upper, lower], axis=1).reshape(NRHS, 2, FINE)
        stores[j].start()
    for store in stores:
        store.wait()


def prolong(vectors, coef):
    return pl.pallas_call(
        prolong_kernel,
        out_shape=jax.ShapeDtypeStruct((SITES, NRHS, 2, FINE), BF),
        in_specs=[pl.BlockSpec(memory_space=pl.ANY), pl.BlockSpec(memory_space=pltpu.VMEM)],
        out_specs=pl.BlockSpec(memory_space=pl.ANY),
        scratch_shapes=[
            pltpu.VMEM((SITES, NRHS, 2, FINE), BF),
            pltpu.VMEM((SITES, NVEC, FINE), BF),
            pltpu.SemaphoreType.DMA((GROUPS,)),
            pltpu.SemaphoreType.DMA((GROUPS,)),
        ],
        compiler_params=pltpu.CompilerParams(vmem_limit_bytes=VMEM_LIMIT),
        name="prolong",
    )(vectors, coef)


def on_device(fine_residual, near_null, coarse_operator):
    fine = fine_residual.reshape(SITES, NRHS, 2, FINE)
    vectors = near_null.reshape(SITES, NVEC, FINE)
    operator = coarse_operator.reshape(GRP, SITES, 64, 9 * COMP)
    coef, residual = solve(fine, vectors, operator)
    fine_correction = prolong(vectors, coef)
    return (
        fine_correction.reshape(fine_residual.shape),
        residual.reshape(fine_residual.shape[:4] + (NRHS, COMP)),
    )


def solution(mesh):
    in_specs = (
        P("grp", "dev", None, None, None, None, None),
        P("grp", "dev", None, None, None, None, None),
        P(None, "dev", None, None, None, None),
    )
    out_specs = (
        P("grp", "dev", None, None, None, None, None),
        P("grp", "dev", None, None, None, None),
    )
    return jax.shard_map(
        on_device, mesh=mesh, in_specs=in_specs, out_specs=out_specs, check_vma=False
    )
```

time: 674 us -> 66.6 us (0.10)
  blocking collectives: 466 us -> 0 us
  local copies, waits for them, and re-layouts: 72.9 us -> 0.68 us
  Pallas kernels: 0 us -> 65 us
  other arithmetic: 48.6 us -> 0 us
  matrix products: 43.4 us -> 0 us
  waiting for transfers between devices: 22.3 us -> 0 us
  starting transfers between devices: 13 us -> 0 us
    psum x5 -> x0, blocking collectives: 456 us -> none  [reduce_terms(): return lax.psum(terms, 'dev')]
    pallas_call x0 -> x2, Pallas kernels: none -> 65 us  [the longest x1 59.6 us: solve(): pl.pallas_call(gcr_kernel, out_shape=(jax.ShapeDtypeStruct((SITES, 2 * NR...]
    dot_general x7 -> x0, matrix products: 43.4 us -> none  [the longest x3 36.3 us: coarse_apply(): jnp.einsum('sidk,sdnqk->snqi', blocks, columns, preferred_element_type=jn...]
    reshape x4 -> x0, local copies, waits for them, and re-layouts: 25.9 us -> none  [the longest x1 19.7 us: coarse_apply(): blocks = operator.reshape(sites_total, ncoarse, 9, 2 * ncoarse)]
    ppermute x6 -> x0, waiting for transfers between devices: 22.3 us -> none  [the longest x3 11.5 us: padded_2(): lax.ppermute(lax.slice_in_dim(block, block.shape[dim] - width, None, axis...]
    concatenate x5 -> x0, other arithmetic: 14.7 us -> none  [the longest x3 11.8 us: complex_columns(): former = jnp.concatenate([real_part, -imag_part], axis=-1)]
    concatenate x6 -> x0, local copies, waits for them, and re-layouts: 14.3 us -> none  [the longest x3 7.21 us: complex_columns(): latter = jnp.concatenate([imag_part, real_part], axis=-1)]
    unnamed x35 -> x3, local copies, waits for them, and re-layouts: 14 us -> 0.68 us
  transfers between devices with their start and end apart: 6 -> 0, of which waited for: 4 -> 0; matrix products, arithmetic and copies ran while one was open for 4% -> 0% of each run, Pallas kernels for 0% -> 0%
where the time goes in v1:
time: 66.6 us; the launch traced here: 66.3 us
  Pallas kernels  65 us (98%)
  local copies, waits for them, and re-layouts  0.68 us (1%)
    pallas_call x1, Pallas kernels, solve(): pl.pallas_call(gcr_kernel, out_shape=(jax.ShapeDtypeStruct((SITES, 2 * NR...  59.6 us
    pallas_call x1, Pallas kernels, prolong(): pl.pallas_call(prolong_kernel, out_shape=jax.ShapeDtypeStruct((SITES, NRH...  5.38 us

profile of v1, /device:TPU:0, one launch (start us, length us, event | category | flops | bytes accessed | tf_op | source)
XLA Modules:
  0.0 66.3 jit_solution(11577890139870056442)
XLA Ops:
  0.6 59.6 %restrict_gcr.1 = (bf16[16,48,128]{2,1,0:T(8,128)(2,1)}, f32[16,24,128]{2,1,0:T(8,128)}) custom-call(bf16[16,24,2,3072]{3,2,1,0:T(2,128)(2,1)} %bitcast.8, bf16[16,64,3072]{2,1,0:T(8,128)(2,1)} %bitcast.5, bf16[4,16,64,1152]{3,2,1,0:T(8,128)(2,1)} %bitcast.7), custom_call_target="tpu_custom_call" | custom-call | tf_op jit(solution)/shard_map/restrict_gcr/pallas_call | solution.py:301
  60.2 0.0 copy-start
  60.2 5.4 %prolong.1 = bf16[16,24,2,3072]{3,2,1,0:T(2,128)(2,1)} custom-call(bf16[16,64,3072]{2,1,0:T(8,128)(2,1)} %bitcast.6, bf16[16,48,128]{2,1,0:T(8,128)(2,1)} %get-tuple-element.4.coef_ref), custom_call_target="tpu_custom_call" | custom-call | tf_op jit(solution)/shard_map/prolong/pallas_call | solution.py:363
  65.6 0.0 copy-done
  65.6 0.7 %copy.6 = f32[1,1,4,4,24,128]{5,4,3,2,1,0:T(8,128)} copy(f32[1,1,4,4,24,128]{5,4,3,2,1,0:T(8,128)S(1)} %bitcast.10) | data formatting | bytes 393216
Async XLA Ops:
  60.2 5.4 %copy-start = (f32[16,24,128]{2,1,0:T(8,128)S(1)}, f32[16,24,128]{2,1,0:T(8,128)}, u32[]{:S(2)}) copy-start(f32[16,24,128]{2,1,0:T(8,128)} %get-tuple-element.5) | copy-start | bytes 589828
